TPU v7x, 512 devices: a whole 4x8x8 slice. The times are simulated.
512 devices in a mesh: seq: 64 (over x, y, z_lo), tp: 8 (over z_hi, core).
Axes of the slice: x: 4, y: 8, z: 8 (z_hi: 4, z_lo: 2; z = z_hi * 2 + z_lo), core: 2. Of those that a mesh axis runs over, the one named last changes fastest.
Arguments:
- queries: bfloat16 [16384, 3072], P(('seq', 'tp')), may hold values from -42 to 42
- keys: bfloat16 [16384, 3072], P(('seq', 'tp')), may hold values from -6 to 6
- values: bfloat16 [16384, 3072], P(('seq', 'tp')), may hold values from -6 to 6
- pool_keys: bfloat16 [64, 128, 3072], P('seq', None, 'tp'), may hold values from -6 to 6
- pool_values: bfloat16 [64, 128, 3072], P('seq', None, 'tp'), may hold values from -6 to 6
- page_table: int32 [64], replicated, may hold values from 0 to 63, each once
- lengths: int32 [128], replicated, may hold values from 1 to 256, 16384 in all
- group_of: int32 [128], replicated, may hold values from 0 to 1
Outputs:
- context: bfloat16 [16384, 3072], P(('seq', 'tp'))
- new_keys: bfloat16 [16384, 3072], P('seq', 'tp')
- new_values: bfloat16 [16384, 3072], P('seq', 'tp')
Inputs may be any that keep to these rules, and one draw needn't show every extreme that they name: `page_table`: each of the 64 slots appears once; entries g * 32 to (g + 1) * 32 - 1 are group g's pages; slot s lies on index s of seq. The lengths sum to 16384; each request's suffix tokens follow those of the requests before it.
All inputs are finite; a program needn't handle non-finite values.
Results may differ from a plain program's by a relative error of at most 0.0055.
Values may be sent and summed in bfloat16 or wider, within the bound.
A program may use at most 64 MiB of HBM per device.

v0:
```python
import math
import jax
import jax.numpy as jnp
from jax import lax
from jax.sharding import PartitionSpec as P

HD = 96
ROT = 24


def shifted(block, axis, distance):
    devices = range(lax.axis_size(axis))
    route = [(i - distance, i) for i in devices if i - distance in devices]
    return lax.ppermute(block, axis, route)


def rotate(matrix, position):
    count = matrix.shape[0]
    split_heads = matrix.reshape(count, -1, HD)
    half_rot = ROT // 2
    inverse_freq = 10000.0 ** (-(jnp.arange(half_rot, dtype=jnp.float32) * 2.0 / ROT))
    angles = position.astype(jnp.float32)[:, None] * inverse_freq[None, :]
    cosine = jnp.cos(angles)[:, None, :]
    sine = jnp.sin(angles)[:, None, :]
    first_half = split_heads[..., :half_rot]
    second_half = split_heads[..., half_rot:ROT]
    rest_dims = split_heads[..., ROT:]
    turned = jnp.concatenate(
        [
            first_half * cosine - second_half * sine,
            second_half * cosine + first_half * sine,
            rest_dims,
        ],
        axis=-1,
    )
    return turned.reshape(count, -1)


def local(queries, keys, values, pool_keys, pool_values, page_table, lengths, group_of):
    seq_count = lax.axis_size("seq")
    head_queries, head_keys, head_values = (
        lax.all_to_all(queries, "tp", split_axis=1, concat_axis=0, tiled=True),
        lax.all_to_all(keys, "tp", split_axis=1, concat_axis=0, tiled=True),
        lax.all_to_all(values, "tp", split_axis=1, concat_axis=0, tiled=True),
    )
    tok_rows = head_queries.shape[0]
    channels = head_queries.shape[1]
    heads_here = channels // HD
    page_rows = pool_keys.shape[1]
    slots_here = pool_keys.shape[0]
    slot_count = slots_here * seq_count
    pages_group = slot_count // 2
    prefix_len = pages_group * page_rows
    request_count = lengths.shape[0]
    request_ends = jnp.cumsum(lengths)
    request_starts = request_ends - lengths
    request_ids = jnp.arange(request_count, dtype=jnp.int32)
    my_index = lax.axis_index("seq")
    row_base = my_index * tok_rows
    query_rows = row_base + jnp.arange(tok_rows, dtype=jnp.int32)
    request = jnp.sum((query_rows[:, None] >= request_ends[None, :]).astype(jnp.int32), axis=1)
    one_hot = (request[:, None] == request_ids[None, :]).astype(jnp.int32)
    offset = query_rows - jnp.sum(one_hot * request_starts[None, :], axis=1)
    group = jnp.sum(one_hot * group_of[None, :], axis=1)
    position = prefix_len + offset
    rot_queries = rotate(head_queries.astype(jnp.float32), position).astype(jnp.bfloat16)
    rot_keys = rotate(head_keys.astype(jnp.float32), position).astype(jnp.bfloat16)
    earlier_keys, earlier_values = shifted((rot_keys, head_values), "seq", 1)
    earlier_rows = query_rows - tok_rows
    earlier_request = jnp.sum(
        (earlier_rows[:, None] >= request_ends[None, :]).astype(jnp.int32), axis=1
    )
    suffix_keys = jnp.concatenate([earlier_keys, rot_keys], axis=0)
    suffix_values = jnp.concatenate([earlier_values, head_values], axis=0)
    key_rows = jnp.concatenate([earlier_rows, query_rows], axis=0)
    key_request = jnp.concatenate([earlier_request, request], axis=0)
    suffix_mask = (
        (key_request[None, :] == request[:, None])
        & (key_rows[None, :] <= query_rows[:, None])
        & (key_rows[None, :] >= 0)
    )
    slot_ids = jnp.arange(slot_count, dtype=jnp.int32)
    member = (page_table[None, :] == slot_ids[:, None]) & (slot_ids[None, :] >= pages_group)
    slot_group = jnp.any(member, axis=1).astype(jnp.int32)
    score_scale = HD ** (-0.5)

    def attend(state, query_block, key_block, value_block, allowed):
        row_max, total, accum = state
        query_heads = query_block.reshape(query_block.shape[0], heads_here, HD)
        key_heads = key_block.reshape(key_block.shape[0], heads_here, HD)
        value_heads = value_block.reshape(value_block.shape[0], heads_here, HD)
        scores = (
            jnp.einsum("qhd,khd->hqk", query_heads, key_heads, preferred_element_type=jnp.float32)
            * score_scale
        )
        scores = jnp.where(allowed[None], scores, -1e30)
        new_max = jnp.maximum(row_max, jnp.max(scores, axis=-1))
        weights = jnp.where(allowed[None], jnp.exp(scores - new_max[..., None]), 0.0)
        factor = jnp.exp(row_max - new_max)
        new_total = total * factor + jnp.sum(weights, axis=-1)
        weights_bf16 = weights.astype(jnp.bfloat16)
        new_accum = accum * factor[..., None] + jnp.einsum(
            "hqk,khd->hqd", weights_bf16, value_heads, preferred_element_type=jnp.float32
        )
        return (new_max, new_total, new_accum)

    initial = (
        jnp.full((heads_here, tok_rows), -1e30, jnp.float32),
        jnp.zeros((heads_here, tok_rows), jnp.float32),
        jnp.zeros((heads_here, tok_rows, HD), jnp.float32),
    )
    state = initial
    piece_keys = lax.all_gather(pool_keys, "seq", axis=0, tiled=True)
    piece_slots = piece_keys.shape[0]
    piece_ids = jnp.arange(piece_slots, dtype=jnp.int32)
    piece_group = jnp.sum(
        (piece_ids[:, None] == slot_ids[None, :]).astype(jnp.int32) * slot_group[None, :], axis=1
    )
    block_pages = math.gcd(piece_slots, 4)
    block_count = piece_slots // block_pages
    keys_blocked = piece_keys.reshape(block_count, block_pages * page_rows, channels)
    values_blocked = lax.all_gather(pool_values, "seq", axis=0, tiled=True).reshape(
        block_count, block_pages * page_rows, channels
    )
    groups_blocked = piece_group.reshape(block_count, block_pages)

    def one_step(running, item):
        key_block, value_block, group_block = item
        key_group = jnp.repeat(group_block, page_rows)
        allowed = group[:, None] == key_group[None, :]
        return (attend(running, rot_queries, key_block, value_block, allowed), None)

    state, _ = lax.scan(one_step, state, (keys_blocked, values_blocked, groups_blocked))
    state = attend(state, rot_queries, suffix_keys, suffix_values, suffix_mask)
    final_max, final_total, final_accum = state
    context_heads = (
        (final_accum / final_total[..., None])
        .transpose(1, 0, 2)
        .reshape(tok_rows, channels)
        .astype(jnp.bfloat16)
    )
    context = lax.all_to_all(context_heads, "tp", split_axis=0, concat_axis=1, tiled=True)
    return (context, rot_keys, head_values)


def solution(mesh):
    return jax.shard_map(
        local,
        mesh=mesh,
        in_specs=(
            P(("seq", "tp"), None),
            P(("seq", "tp"), None),
            P(("seq", "tp"), None),
            P("seq", None, "tp"),
            P("seq", None, "tp"),
            P(),
            P(),
            P(),
        ),
        out_specs=(P(("seq", "tp"), None), P("seq", "tp"), P("seq", "tp")),
        check_vma=False,
    )
```

profile of v0, /device:TPU:1, one launch (start us, length us, event | category | flops | bytes accessed | tf_op | source)
XLA Modules:
  0.0 726.4 jit_solution(3364903707367896653)
XLA Ops:
  7.2 0.7 all-gather.3.cloned.1.call-update
  8.0 0.7 all-gather.5.cloned.1.call-update
  8.7 1.6 copy.109
  10.3 11.8 %all-to-all-start = ((bf16[32,8,384]{2,0,1:T(8,128)(2,1)}), bf16[32,8,384]{2,0,1:T(8,128)(2,1)S(1)}, u32[]{:S(2)}, u32[]{:S(2)}) async-start(bf16[32,8,384]{2,0,1:T(8,128)(2,1)} %bitcast.52), calls=%async_computation | async-start | bytes 393216 | tf_op jit(solution)/shard_map/all_to_all | solution.py:42
  22.1 0.8 copy.76
  23.1 0.7 sub.42
  24.1 0.9 select_reduce_fusion.1
  25.0 1.6 copy.108
  26.6 0.8 fusion.28
  27.5 4.6 all-to-all-done
  32.1 4.6 all-to-all-start.1
  36.8 0.7 copy.107
  37.7 12.3 %all-to-all-done.1 = bf16[32,8,384]{2,0,1:T(8,128)(2,1)S(1)} async-done(((bf16[32,8,384]{2,0,1:T(8,128)(2,1)}), bf16[32,8,384]{2,0,1:T(8,128)(2,1)S(1)}, u32[]{:S(2)}, u32[]{:S(2)}) %all-to-all-start.1) | async-done | bytes 196640 | tf_op jit(solution)/shard_map/all_to_all | solution.py:43
  50.0 3.7 all-to-all-start.2
  54.8 9.4 %all-to-all-done.2 = bf16[32,8,384]{2,0,1:T(8,128)(2,1)S(1)} async-done(((bf16[32,8,384]{2,0,1:T(8,128)(2,1)}), bf16[32,8,384]{2,0,1:T(8,128)(2,1)S(1)}, u32[]{:S(2)}, u32[]{:S(2)}) %all-to-all-start.2) | async-done | bytes 196640 | tf_op jit(solution)/shard_map/all_to_all | solution.py:44
  64.3 3.8 collective-permute-start.1
  68.5 0.6 pad_maximum_fusion.1
  69.3 3.3 collective-permute-start
  74.4 5.3 collective-permute-done
  79.7 1.9 fusion.13
  81.7 207.7 %all-gather.3.cloned.1.call-done = bf16[64,128,384]{2,1,0:T(8,128)(2,1)} async-done(((bf16[1,128,384]{2,1,0:T(8,128)(2,1)}), bf16[64,128,384]{2,1,0:T(8,128)(2,1)}) %all-gather.3.cloned.1.call-update) | async-done | bytes 6291472 | tf_op jit(solution)/shard_map/all_gather | solution.py:113
  289.4 305.0 %all-gather.5.cloned.1.call-done = bf16[64,128,384]{2,1,0:T(8,128)(2,1)} async-done(((bf16[1,128,384]{2,1,0:T(8,128)(2,1)}), bf16[64,128,384]{2,1,0:T(8,128)(2,1)}) %all-gather.5.cloned.1.call-update) | async-done | bytes 6291472 | tf_op jit(solution)/shard_map/all_gather | solution.py:122
  594.4 59.1 %while.15 = (s32[]{:T(128)}, f32[4,256]{1,0:T(4,128)S(1)}, f32[4,256]{1,0:T(4,128)S(1)}, f32[4,256,96]{1,2,0:T(8,128)S(1)}, s32[256]{0:T(256)S(1)}, /*index=5*/s...) while((s32[]{:T(128)}, f32[4,256]{1,0:T(4,128)S(1)}, ...), condition=%wide.region_9.10_spmd.clone, body=%wide.region_6.0_spmd.clone.sunk | while | flops 208573440 | bytes 11801785 | solution.py:133
  594.6 1.2 constant_dynamic-slice_fusion.4
  597.3 0.7 convolution_add_fusion.3
  598.3 1.2 constant_dynamic-slice_fusion.4
  601.0 0.7 convolution_add_fusion.3
  602.0 1.2 constant_dynamic-slice_fusion.4
  603.6 0.6 fusion.53
  604.7 0.7 convolution_add_fusion.3
  605.7 1.2 constant_dynamic-slice_fusion.4
  608.4 0.7 convolution_add_fusion.3
  609.4 1.2 constant_dynamic-slice_fusion.4
  612.1 0.7 convolution_add_fusion.3
  613.1 1.2 constant_dynamic-slice_fusion.4
  615.8 0.7 convolution_add_fusion.3
  616.8 1.2 constant_dynamic-slice_fusion.4
  619.5 0.7 convolution_add_fusion.3
  620.5 1.2 constant_dynamic-slice_fusion.4
  623.2 0.7 convolution_add_fusion.3
  624.2 1.2 constant_dynamic-slice_fusion.4
  626.9 0.7 convolution_add_fusion.3
  627.9 1.2 constant_dynamic-slice_fusion.4
  630.6 0.7 convolution_add_fusion.3
  631.6 1.2 constant_dynamic-slice_fusion.4
  634.3 0.7 convolution_add_fusion.3
  635.3 1.2 constant_dynamic-slice_fusion.4
  638.0 0.7 convolution_add_fusion.3
  639.0 1.2 constant_dynamic-slice_fusion.4
  641.7 0.7 convolution_add_fusion.3
  642.7 1.2 constant_dynamic-slice_fusion.4
  645.4 0.7 convolution_add_fusion.3
  646.4 1.2 constant_dynamic-slice_fusion.4
  649.1 0.7 convolution_add_fusion.3
  650.1 1.2 constant_dynamic-slice_fusion.4
  652.8 0.7 convolution_add_fusion.3
  653.6 2.5 fusion.14
  656.1 0.8 fusion.18
  657.1 0.9 convert_element_type.86
  658.0 50.2 %all-to-all-start.3 = ((bf16[8,32,384]{2,1,0:T(8,128)(2,1)}), bf16[8,32,384]{2,1,0:T(8,128)(2,1)S(1)}, u32[]{:S(2)}, u32[]{:S(2)}) async-start(bf16[8,32,384]{2,1,0:T(8,128)(2,1)} %convert_element_type.86), calls=%async_computation.3 | async-start | bytes 393216 | tf_op jit(solution)/shard_map/all_to_all | solution.py:142
  708.1 0.8 copy.93
  708.9 9.2 %all-to-all-done.3 = bf16[8,32,384]{2,1,0:T(8,128)(2,1)S(1)} async-done(((bf16[8,32,384]{2,1,0:T(8,128)(2,1)}), bf16[8,32,384]{2,1,0:T(8,128)(2,1)S(1)}, u32[]{:S(2)}, u32[]{:S(2)}) %all-to-all-start.3) | async-done | bytes 196640 | tf_op jit(solution)/shard_map/all_to_all | solution.py:142
  718.2 0.7 copy.103
  718.9 0.7 copy.127
  (208 shorter events, 31.5 us)
Async XLA Ops:
  7.2 29.6 %copy-start.1 = (bf16[32,3072]{1,0:T(8,128)(2,1)S(1)}, bf16[32,3072]{1,0:T(8,128)(2,1)}, u32[]{:S(2)}) copy-start(bf16[32,3072]{1,0:T(8,128)(2,1)} %param.12) | copy-start | bytes 589828
  7.2 282.2 %all-gather.3.cloned.1.call-start = ((), (), s32[]{:S(2)}) async-start(), calls=%async_computation.4 | async-start | bytes 6389760 | tf_op jit(solution)/shard_map/all_gather | solution.py:113
  7.9 586.5 %all-gather.5.cloned.1.call-start = ((), (), s32[]{:S(2)}) async-start(), calls=%async_computation.5 | async-start | bytes 6389760 | tf_op jit(solution)/shard_map/all_gather | solution.py:122
  10.3 21.8 %all-to-all-start = ((bf16[32,8,384]{2,0,1:T(8,128)(2,1)}), bf16[32,8,384]{2,0,1:T(8,128)(2,1)S(1)}, u32[]{:S(2)}, u32[]{:S(2)}) async-start(bf16[32,8,384]{2,0,1:T(8,128)(2,1)} %bitcast.52), calls=%async_computation | async-start | bytes 393216 | tf_op jit(solution)/shard_map/all_to_all | solution.py:42
  32.1 17.9 %all-to-all-start.1 = ((bf16[32,8,384]{2,0,1:T(8,128)(2,1)}), bf16[32,8,384]{2,0,1:T(8,128)(2,1)S(1)}, u32[]{:S(2)}, u32[]{:S(2)}) async-start(bf16[32,8,384]{2,0,1:T(8,128)(2,1)} %bitcast.51), calls=%async_computation.1 | async-start | bytes 393216 | tf_op jit(solution)/shard_map/all_to_all | solution.py:43
  50.0 14.3 %all-to-all-start.2 = ((bf16[32,8,384]{2,0,1:T(8,128)(2,1)}), bf16[32,8,384]{2,0,1:T(8,128)(2,1)S(1)}, u32[]{:S(2)}, u32[]{:S(2)}) async-start(bf16[32,8,384]{2,0,1:T(8,128)(2,1)} %bitcast.50), calls=%async_computation.2 | async-start | bytes 393216 | tf_op jit(solution)/shard_map/all_to_all | solution.py:44
  64.3 9.9 %collective-permute-start.1 = (bf16[256,384]{1,0:T(8,128)(2,1)S(1)}, bf16[256,384]{1,0:T(8,128)(2,1)S(1)}, u32[]{:S(2)}, u32[]{:S(2)}) collective-permute-start(bf16[256,384]{1,0:T(8,128)(2,1)S(1)} %bitcast.79), channel_id=1, source_target_pairs={{0,8},{8,16},{16,24},{24,32},{32,40},{40,48},{48,56},{56,64},{64,7... | collective-permute-start | bytes 589832 | tf_op jit(solution)/shard_map/ppermute | solution.py:14
  69.3 10.4 %collective-permute-start = (bf16[256,384]{0,1:T(8,128)(2,1)S(1)}, bf16[256,384]{0,1:T(8,128)(2,1)S(1)}, u32[]{:S(2)}, u32[]{:S(2)}) collective-permute-start(bf16[256,384]{0,1:T(8,128)(2,1)S(1)} %bitcast.82), channel_id=1, source_target_pairs={{0,8},{8,16},{16,24},{24,32},{32,40},{40,48},{48,56},{56,64},{64,7... | collective-permute-start | bytes 589832 | tf_op jit(solution)/shard_map/ppermute | solution.py:14
  653.5 2.6 copy-start
  658.0 60.2 %all-to-all-start.3 = ((bf16[8,32,384]{2,1,0:T(8,128)(2,1)}), bf16[8,32,384]{2,1,0:T(8,128)(2,1)S(1)}, u32[]{:S(2)}, u32[]{:S(2)}) async-start(bf16[8,32,384]{2,1,0:T(8,128)(2,1)} %convert_element_type.86), calls=%async_computation.3 | async-start | bytes 393216 | tf_op jit(solution)/shard_map/all_to_all | solution.py:142
Sparse Core Ops, SparseCore 0:
  10.1 279.2 all-gather.2
  291.5 302.8 all-gather.4
where the time goes:
time: 727 us; the launch traced here: 726 us
  waiting for transfers between devices  555 us (76%)
  starting transfers between devices  77.5 us (11%)
  local copies, waits for them, and re-layouts  37.7 us (5%)
  matrix products  22.9 us (3%)
  other arithmetic  17.8 us (2%)
  between operations  14.3 us (2%)
    all_gather x1, waiting for transfers between devices, local(): lax.all_gather(pool_values, 'seq', axis=0, tiled=True)  305 us
    all_gather x1, waiting for transfers between devices, local(): piece_keys = lax.all_gather(pool_keys, 'seq', axis=0, tiled=True)  208 us
    all_to_all x1, starting transfers between devices, local(): lax.all_to_all(context_heads, 'tp', split_axis=0, concat_axis=1, tiled=True)  50.2 us
    dynamic_slice x48, local copies, waits for them, and re-layouts, local(): lax.scan(one_step, state, (keys_blocked, values_blocked, groups_blocked))  25.3 us
  transfers between devices with their start and end apart: 8, of which 7 were waited for; matrix products, arithmetic and copies ran while one was open for 2% of the time, Pallas kernels for 0%

commit v1 on v0

--- a/solution.py
+++ b/solution.py
@@ -110,7 +110,10 @@
         jnp.zeros((heads_here, tok_rows, HD), jnp.float32),
     )
     state = initial
-    piece_keys = lax.all_gather(pool_keys, "seq", axis=0, tiled=True)
+    n_dev = lax.axis_size("seq")
+    parts = jnp.stack([pool_keys for _ in range(n_dev)])
+    parts = lax.all_to_all(parts, "seq", split_axis=0, concat_axis=0)
+    piece_keys = jnp.concatenate(parts, axis=0)
     piece_slots = piece_keys.shape[0]
     piece_ids = jnp.arange(piece_slots, dtype=jnp.int32)
     piece_group = jnp.sum(

time: 727 us -> 564 us (0.78)
  waiting for transfers between devices: 555 us -> 322 us
  matrix products: 22.9 us -> 51.3 us
  local copies, waits for them, and re-layouts: 37.7 us -> 53.8 us
  blocking collectives: 0 us -> 13.1 us
  other arithmetic: 17.8 us -> 27.4 us
    all_gather x1 -> x0, waiting for transfers between devices: 208 us -> none  [local(): piece_keys = lax.all_gather(pool_keys, 'seq', axis=0, tiled=True)]
    all_gather x1, waiting for transfers between devices: 305 us -> 147 us  [local(): lax.all_gather(pool_values, 'seq', axis=0, tiled=True)]
    all_to_all x1, waiting for transfers between devices: 9.43 us -> 128 us  [local(): parts = lax.all_to_all(parts, 'seq', split_axis=0, concat_axis=0)]
    dot_general x17, matrix products: 12.1 us -> 39.9 us  [attend(): jnp.einsum('hqk,khd->hqd', weights_bf16, value_heads, preferred_element_t...]
    ppermute x2, waiting for transfers between devices: 5.34 us -> 22.5 us  [shifted(): return lax.ppermute(block, axis, route)]
    all_to_all x0 -> x1, blocking collectives: none -> 13.1 us  [local(): lax.all_to_all(values, 'tp', split_axis=1, concat_axis=0, tiled=True)]
    squeeze x16, local copies, waits for them, and re-layouts: 0.15 us -> 10.8 us  [local(): lax.scan(one_step, state, (keys_blocked, values_blocked, groups_blocked))]
    eq x16, other arithmetic: 2.29 us -> 12.7 us  [one_step(): allowed = group[:, None] == key_group[None, :]]
  transfers between devices with their start and end apart: 8 -> 7, of which waited for: 7 -> 6; matrix products, arithmetic and copies ran while one was open for 2% -> 2% of each run, Pallas kernels for 0% -> 0%
where the time goes in v1:
time: 564 us; the launch traced here: 562 us
  waiting for transfers between devices  322 us (57%)
  starting transfers between devices  78.7 us (14%)
  local copies, waits for them, and re-layouts  53.8 us (10%)
  matrix products  51.3 us (9%)
  other arithmetic  27.4 us (5%)
  between operations  14.3 us (3%)
  blocking collectives  13.1 us (2%)
    all_gather x1, waiting for transfers between devices, local(): lax.all_gather(pool_values, 'seq', axis=0, tiled=True)  147 us
    all_to_all x1, waiting for transfers between devices, local(): parts = lax.all_to_all(parts, 'seq', split_axis=0, concat_axis=0)  128 us
    all_to_all x1, starting transfers between devices, local(): lax.all_to_all(context_heads, 'tp', split_axis=0, concat_axis=1, tiled=True)  44.3 us
    dot_general x17, matrix products, attend(): jnp.einsum('hqk,khd->hqd', weights_bf16, value_heads, preferred_element_t...  39.9 us
    dynamic_slice x48, local copies, waits for them, and re-layouts, local(): lax.scan(one_step, state, (keys_blocked, values_blocked, groups_blocked))  25.4 us
    ppermute x2, waiting for transfers between devices, shifted(): return lax.ppermute(block, axis, route)  22.5 us
    all_to_all x1, blocking collectives, local(): lax.all_to_all(values, 'tp', split_axis=1, concat_axis=0, tiled=True)  13.1 us
    eq x16, other arithmetic, one_step(): allowed = group[:, None] == key_group[None, :]  12.7 us
  transfers between devices with their start and end apart: 7, of which 6 were waited for; matrix products, arithmetic and copies ran while one was open for 2% of the time, Pallas kernels for 0%

profile of v1, /device:TPU:1, one launch (start us, length us, event | category | flops | bytes accessed | tf_op | source)
XLA Modules:
  0.0 561.6 jit_solution(2506320380217209732)
XLA Ops:
  7.2 1.7 copy.108
  8.8 11.8 %all-to-all-start.2 = ((bf16[32,8,384]{2,0,1:T(8,128)(2,1)}), bf16[32,8,384]{2,0,1:T(8,128)(2,1)S(1)}, u32[]{:S(2)}, u32[]{:S(2)}) async-start(bf16[32,8,384]{2,0,1:T(8,128)(2,1)} %bitcast.52), calls=%async_computation.2 | async-start | bytes 393216 | tf_op jit(solution)/shard_map/all_to_all | solution.py:43
  20.6 1.6 copy.109
  22.2 8.4 %all-to-all-done.2 = bf16[32,8,384]{2,0,1:T(8,128)(2,1)S(1)} async-done(((bf16[32,8,384]{2,0,1:T(8,128)(2,1)}), bf16[32,8,384]{2,0,1:T(8,128)(2,1)S(1)}, u32[]{:S(2)}, u32[]{:S(2)}) %all-to-all-start.2) | async-done | bytes 196640 | tf_op jit(solution)/shard_map/all_to_all | solution.py:43
  30.6 4.6 all-to-all-start.1
  35.2 0.9 copy.107
  36.2 7.7 %all-to-all-done.1 = bf16[32,8,384]{2,0,1:T(8,128)(2,1)S(1)} async-done(((bf16[32,8,384]{2,0,1:T(8,128)(2,1)}), bf16[32,8,384]{2,0,1:T(8,128)(2,1)S(1)}, u32[]{:S(2)}, u32[]{:S(2)}) %all-to-all-start.1) | async-done | bytes 196640 | tf_op jit(solution)/shard_map/all_to_all | solution.py:42
  43.9 13.1 %all_to_all.66 = bf16[32,8,384]{2,0,1:T(8,128)(2,1)S(1)} all-to-all(bf16[32,8,384]{2,0,1:T(8,128)(2,1)S(1)} %bitcast.89), channel_id=1, replica_groups=mesh['seq'=64,'tp'=8] {'tp'}, dimensions={1} | all-to-all | bytes 393216 | tf_op jit(solution)/shard_map/all_to_all | solution.py:44
  57.0 3.6 stack.2
  60.6 12.0 %all-to-all-start = ((bf16[64,1,128,384]{3,2,1,0:T(8,128)(2,1)}), bf16[64,1,128,384]{3,2,1,0:T(8,128)(2,1)}, u32[]{:S(2)}, u32[]{:S(2)}) async-start(bf16[64,1,128,384]{3,2,1,0:T(8,128)(2,1)} %stack.2), calls=%async_computation | async-start | bytes 12582912 | tf_op jit(solution)/shard_map/all_to_all | solution.py:115
  78.0 2.9 collective-permute-start
  82.0 3.1 collective-permute-start.1
  85.7 0.8 copy.90
  86.6 22.5 %collective-permute-done.1 = bf16[256,384]{1,0:T(8,128)(2,1)S(1)} collective-permute-done((bf16[256,384]{1,0:T(8,128)(2,1)S(1)}, bf16[256,384]{1,0:T(8,128)(2,1)S(1)}, u32[]{:S(2)}, u32[]{:S(2)}) %collective-permute-start.1) | collective-permute-done | bytes 196640 | tf_op jit(solution)/shard_map/ppermute | solution.py:14
  109.2 0.8 copy.89
  110.0 2.5 fusion.13
  112.5 128.2 %all-to-all-done = bf16[64,1,128,384]{3,2,1,0:T(8,128)(2,1)} async-done(((bf16[64,1,128,384]{3,2,1,0:T(8,128)(2,1)}), bf16[64,1,128,384]{3,2,1,0:T(8,128)(2,1)}, u32[]{:S(2)}, u32[]{:S(2)}) %all-to-all-start) | async-done | bytes 6291488 | tf_op jit(solution)/shard_map/all_to_all | solution.py:115
  240.6 146.9 %all-gather.2.cloned.1.call-done = bf16[64,128,384]{2,1,0:T(8,128)(2,1)} async-done(((bf16[1,128,384]{2,1,0:T(8,128)(2,1)}), bf16[64,128,384]{2,1,0:T(8,128)(2,1)}) %all-gather.2.cloned.1.call-update) | async-done | bytes 6291472 | tf_op jit(solution)/shard_map/all_gather | solution.py:125
  387.6 106.5 %while.15 = (s32[]{:T(128)}, f32[4,256]{1,0:T(4,128)S(1)}, f32[4,256]{1,0:T(4,128)S(1)}, f32[4,256,96]{1,2,0:T(8,128)}, s32[256]{0:T(256)}, /*index=5*/s32[16,4]...) while((s32[]{:T(128)}, f32[4,256]{1,0:T(4,128)S(1)}, ...), condition=%wide.region_9.10_spmd.clone, body=%wide.region_6.0_spmd.clone.sunk | while | flops 208573440 | bytes 11801777 | solution.py:136
  388.3 0.8 broadcast_compare_fusion.3
  389.1 1.2 constant_dynamic-slice_fusion.4
  391.9 1.4 convolution_add_fusion.3
  394.1 0.8 broadcast_compare_fusion.3
  394.9 1.2 constant_dynamic-slice_fusion.4
  397.6 2.4 convolution_add_fusion.3
  400.8 0.8 broadcast_compare_fusion.3
  401.6 1.2 constant_dynamic-slice_fusion.4
  404.3 2.4 convolution_add_fusion.3
  407.5 0.8 broadcast_compare_fusion.3
  408.3 1.2 constant_dynamic-slice_fusion.4
  411.0 2.4 convolution_add_fusion.3
  414.2 0.8 broadcast_compare_fusion.3
  415.0 1.2 constant_dynamic-slice_fusion.4
  417.8 2.4 convolution_add_fusion.3
  420.9 0.8 broadcast_compare_fusion.3
  421.7 1.2 constant_dynamic-slice_fusion.4
  424.5 2.4 convolution_add_fusion.3
  428.5 1.2 constant_dynamic-slice_fusion.4
  431.2 2.4 convolution_add_fusion.3
  435.2 1.2 constant_dynamic-slice_fusion.4
  437.9 2.4 convolution_add_fusion.3
  441.9 1.2 constant_dynamic-slice_fusion.4
  444.6 2.4 convolution_add_fusion.3
  448.6 1.2 constant_dynamic-slice_fusion.4
  451.4 2.4 convolution_add_fusion.3
  455.3 1.2 constant_dynamic-slice_fusion.4
  458.1 2.4 convolution_add_fusion.3
  462.1 1.2 constant_dynamic-slice_fusion.4
  464.8 2.4 convolution_add_fusion.3
  468.8 1.2 constant_dynamic-slice_fusion.4
  471.5 2.4 convolution_add_fusion.3
  475.5 1.2 constant_dynamic-slice_fusion.4
  478.2 2.4 convolution_add_fusion.3
  482.2 1.2 constant_dynamic-slice_fusion.4
  485.0 2.4 convolution_add_fusion.3
  488.9 1.2 constant_dynamic-slice_fusion.4
  491.7 2.4 convolution_add_fusion.3
  494.1 0.8 max.6
  495.0 2.4 fusion.14
  497.4 2.0 fusion.18
  499.6 0.9 convert_element_type.86
  500.4 44.3 %all-to-all-start.4 = ((bf16[8,32,384]{2,1,0:T(8,128)(2,1)}), bf16[8,32,384]{2,1,0:T(8,128)(2,1)S(1)}, u32[]{:S(2)}, u32[]{:S(2)}) async-start(bf16[8,32,384]{2,1,0:T(8,128)(2,1)} %convert_element_type.86), calls=%async_computation.4 | async-start | bytes 393216 | tf_op jit(solution)/shard_map/all_to_all | solution.py:145
  544.8 0.8 copy.93
  545.6 7.8 %all-to-all-done.4 = bf16[8,32,384]{2,1,0:T(8,128)(2,1)S(1)} async-done(((bf16[8,32,384]{2,1,0:T(8,128)(2,1)}), bf16[8,32,384]{2,1,0:T(8,128)(2,1)S(1)}, u32[]{:S(2)}, u32[]{:S(2)}) %all-to-all-start.4) | async-done | bytes 196640 | tf_op jit(solution)/shard_map/all_to_all | solution.py:145
  (217 shorter events, 52.5 us)
Async XLA Ops:
  7.2 49.8 %copy-start.3 = (bf16[1,128,384]{2,1,0:T(8,128)(2,1)S(1)}, bf16[1,128,384]{2,1,0:T(8,128)(2,1)}, u32[]{:S(2)}) copy-start(bf16[1,128,384]{2,1,0:T(8,128)(2,1)} %param.13) | copy-start | bytes 294916
  8.8 21.8 %all-to-all-start.2 = ((bf16[32,8,384]{2,0,1:T(8,128)(2,1)}), bf16[32,8,384]{2,0,1:T(8,128)(2,1)S(1)}, u32[]{:S(2)}, u32[]{:S(2)}) async-start(bf16[32,8,384]{2,0,1:T(8,128)(2,1)} %bitcast.52), calls=%async_computation.2 | async-start | bytes 393216 | tf_op jit(solution)/shard_map/all_to_all | solution.py:43
  30.6 13.3 %all-to-all-start.1 = ((bf16[32,8,384]{2,0,1:T(8,128)(2,1)}), bf16[32,8,384]{2,0,1:T(8,128)(2,1)S(1)}, u32[]{:S(2)}, u32[]{:S(2)}) async-start(bf16[32,8,384]{2,0,1:T(8,128)(2,1)} %bitcast.53), calls=%async_computation.1 | async-start | bytes 393216 | tf_op jit(solution)/shard_map/all_to_all | solution.py:42
  60.6 12.8 %copy-start.4 = (s32[128]{0:T(128)S(1)}, s32[128]{0:T(128)}, u32[]{:S(2)}) copy-start(s32[128]{0:T(128)} %param.16) | copy-start | bytes 1540
  60.6 13.3 %copy-start.6 = (s32[64]{0:T(128)S(1)}, s32[64]{0:T(128)}, u32[]{:S(2)}) copy-start(s32[64]{0:T(128)} %param.15) | copy-start | bytes 772
  60.6 14.5 %copy-start.5 = (s32[128]{0:T(128)S(1)}, s32[128]{0:T(128)}, u32[]{:S(2)}) copy-start(s32[128]{0:T(128)} %param.17) | copy-start | bytes 1540
  60.6 180.0 %all-to-all-start = ((bf16[64,1,128,384]{3,2,1,0:T(8,128)(2,1)}), bf16[64,1,128,384]{3,2,1,0:T(8,128)(2,1)}, u32[]{:S(2)}, u32[]{:S(2)}) async-start(bf16[64,1,128,384]{3,2,1,0:T(8,128)(2,1)} %stack.2), calls=%async_computation | async-start | bytes 12582912 | tf_op jit(solution)/shard_map/all_to_all | solution.py:115
  72.6 314.9 %all-gather.2.cloned.1.call-start = ((), (), s32[]{:S(2)}) async-start(), calls=%async_computation.5 | async-start | bytes 6389760 | tf_op jit(solution)/shard_map/all_gather | solution.py:125
  78.0 31.9 %copy-start.1 = (bf16[256,4,96]{0,2,1:T(8,128)(2,1)}, bf16[256,4,96]{0,2,1:T(8,128)(2,1)S(1)}, u32[]{:S(2)}) copy-start(bf16[256,4,96]{0,2,1:T(8,128)(2,1)S(1)} %copy.87) | copy-start | bytes 589828
  78.0 31.9 %collective-permute-start = (bf16[256,384]{0,1:T(8,128)(2,1)S(1)}, bf16[256,384]{0,1:T(8,128)(2,1)S(1)}, u32[]{:S(2)}, u32[]{:S(2)}) collective-permute-start(bf16[256,384]{0,1:T(8,128)(2,1)S(1)} %bitcast.83), channel_id=1, source_target_pairs={{0,8},{8,16},{16,24},{24,32},{32,40},{40,48},{48,56},{56,64},{64,7... | collective-permute-start | bytes 589832 | tf_op jit(solution)/shard_map/ppermute | solution.py:14
  82.0 27.1 %collective-permute-start.1 = (bf16[256,384]{1,0:T(8,128)(2,1)S(1)}, bf16[256,384]{1,0:T(8,128)(2,1)S(1)}, u32[]{:S(2)}, u32[]{:S(2)}) collective-permute-start(bf16[256,384]{1,0:T(8,128)(2,1)S(1)} %bitcast.80), channel_id=1, source_target_pairs={{0,8},{8,16},{16,24},{24,32},{32,40},{40,48},{48,56},{56,64},{64,7... | collective-permute-start | bytes 589832 | tf_op jit(solution)/shard_map/ppermute | solution.py:14
  494.1 3.2 copy-start
  497.4 47.4 %copy-start.2 = (bf16[256,4,96]{0,2,1:T(8,128)(2,1)S(1)}, bf16[256,4,96]{0,2,1:T(8,128)(2,1)}, u32[]{:S(2)}) copy-start(bf16[256,4,96]{0,2,1:T(8,128)(2,1)} %copy-done.1) | copy-start | bytes 589828
  500.4 52.9 %all-to-all-start.4 = ((bf16[8,32,384]{2,1,0:T(8,128)(2,1)}), bf16[8,32,384]{2,1,0:T(8,128)(2,1)S(1)}, u32[]{:S(2)}, u32[]{:S(2)}) async-start(bf16[8,32,384]{2,1,0:T(8,128)(2,1)} %convert_element_type.86), calls=%async_computation.4 | async-start | bytes 393216 | tf_op jit(solution)/shard_map/all_to_all | solution.py:145
Sparse Core Ops, SparseCore 0:
  75.5 312.0 all-gather.1
